TPU v7x, 256 devices: a whole 4x4x8 slice. The times are simulated.
256 devices in a mesh: rows: 64 (over y, z, core), feat: 4 (over x).
Axes of the slice: x: 4, y: 4, z: 8, core: 2. Of those that a mesh axis runs over, the one named last changes fastest.
Arguments:
- cells: bfloat16 [8192, 80, 128], P('rows', 'feat'), may hold values from -19 to 19
- block_table: int32 [64], replicated, may hold values from 0 to 7, as said below
- row_live: int32 [8192], replicated, may hold values from 0 to 1, as said below
- row_train: int32 [8192], replicated, may hold values from 0 to 1, as said below
- feat_qkv: bfloat16 [128, 384], replicated, may hold values from -0.5 to 0.5
- feat_out: bfloat16 [128, 128], replicated, may hold values from -0.5 to 0.5
- item_qkv: bfloat16 [128, 384], replicated, may hold values from -0.5 to 0.5
- item_out: bfloat16 [128, 128], replicated, may hold values from -0.5 to 0.5
Outputs:
- layer_output: bfloat16 [8192, 80, 128], P(('rows', 'feat'))
Inputs may be any that keep to these rules, and one draw needn't show every extreme that they name: `block_table`: every table number appears in some block. `row_live`: every training row is live. `row_train`: each aligned group of 32 rows holds 1 to 4 training rows; some group holds exactly 4.
All inputs are finite; a program needn't handle non-finite values.
Results may differ from a plain program's by a relative error of at most 0.014.
Values may be sent and summed in bfloat16 or wider, within the bound.
A program may use at most 64 MiB of HBM per device.

v0:
```python
import jax
import jax.numpy as jnp
from jax import lax
from jax.sharding import PartitionSpec as P

HEADS = 4
HEAD_DIM = 32
KEEP = 4
TABLES = 8
EPSILON = 1e-05
MASKED = -1e30


def from_everyone(shard, axis):
    peers = lax.axis_size(axis)
    return lax.all_to_all(
        jnp.broadcast_to(shard[None], (peers, *shard.shape)), axis, 0, 0, tiled=True
    )


def of_everyone(shard, axis):
    everything = from_everyone(shard, axis)
    return jnp.sum(everything, axis=0)


def in_one(arrays, axis):
    vector, at, done = (jnp.concatenate([a.reshape(-1) for a in arrays]), 0, [])
    so_far = of_everyone(vector, axis)
    for a in arrays:
        done.append(so_far[at : at + a.size].reshape(a.shape))
        at += a.size
    return tuple(done)


def laid_out(parts, dim):
    lengths = list(parts.shape[1:])
    lengths[dim] *= parts.shape[0]
    return jnp.moveaxis(parts, 0, dim).reshape(lengths)


def gather_together(arrays, axis, dims):
    vector = jnp.concatenate([a.reshape(-1) for a in arrays])
    lines, at, done = (lax.all_gather(vector, axis), 0, [])
    for a, dim in zip(arrays, dims):
        parts = lines[:, at : at + a.size].reshape(-1, *a.shape)
        done.append(laid_out(parts, dim))
        at += a.size
    return tuple(done)


def compact_train(train_rows):
    positions = jnp.arange(train_rows.shape[-1], dtype=jnp.int32)
    ordinal = jnp.cumsum(train_rows, axis=-1) - 1
    slot_ids = jnp.arange(KEEP, dtype=jnp.int32)
    matched = (train_rows[..., None, :] == 1) & (ordinal[..., None, :] == slot_ids[:, None])
    return jnp.sum(jnp.where(matched, positions, 0), axis=-1)


def into_heads(tensor):
    return tensor.reshape(tensor.shape[:-1] + (HEADS, HEAD_DIM))


def attend_features(queries, key_part, value_part):
    row_count, query_feats = (queries.shape[0], queries.shape[1])
    blocks = max(1, row_count * query_feats // 1280)
    while row_count % blocks:
        blocks -= 1
    scaling = HEAD_DIM ** (-0.5)

    def attend_one_block(block_parts):
        block_query, block_key, block_value = block_parts
        scores = (
            jnp.einsum(
                "rqhd,rkhd->rhqk", block_query, block_key, preferred_element_type=jnp.float32
            )
            * scaling
        )
        shares = jax.nn.softmax(scores, axis=-1).astype(jnp.bfloat16)
        return jnp.einsum(
            "rhqk,rkhd->rqhd", shares, block_value, preferred_element_type=jnp.float32
        ).astype(jnp.bfloat16)

    def by_block(tensor):
        return tensor.reshape((blocks, row_count // blocks) + tensor.shape[1:])

    result = lax.map(
        attend_one_block, (by_block(queries), by_block(key_part), by_block(value_part))
    )
    return result.reshape(row_count, query_feats, HEADS * HEAD_DIM)


def feature_layer(normed_cells, feat_out, key_part, value_part, queries):
    attended = attend_features(queries, key_part, value_part)
    update = jnp.dot(attended, feat_out, preferred_element_type=jnp.float32)
    return (normed_cells.astype(jnp.float32) + update).astype(jnp.bfloat16)


def on_device(cells, block_table, row_live, row_train, feat_qkv, feat_out, item_qkv, item_out):
    rows_here, feats_here, width_all = cells.shape
    row_index = lax.axis_index("rows")
    feat_index = lax.axis_index("feat")
    row_devices = lax.axis_size("rows")
    feat_devices = lax.axis_size("feat")
    my_table = lax.dynamic_index_in_dim(block_table, row_index, keepdims=False)
    live_rows = lax.dynamic_slice_in_dim(row_live, row_index * rows_here, rows_here).astype(
        jnp.float32
    )
    values = cells.astype(jnp.float32)
    table_hot = (jnp.arange(TABLES, dtype=jnp.int32) == my_table).astype(jnp.float32)
    first_local = jnp.sum(values * live_rows[:, None, None], axis=(0, 2))
    count_local = jnp.sum(live_rows) * width_all
    second_local = jnp.sum(values * values * live_rows[:, None, None], axis=(0, 2))
    first_sum, second_sum, count_sum = in_one(
        (
            table_hot[:, None] * first_local[None, :],
            table_hot[:, None] * second_local[None, :],
            table_hot * count_local,
        ),
        "rows",
    )
    table_mean = first_sum / count_sum[:, None]
    table_spread = second_sum / count_sum[:, None] - table_mean * table_mean
    mine_mean = lax.dynamic_index_in_dim(table_mean, my_table, keepdims=False)
    centred = values - mine_mean[None, :, None]
    mine_spread = lax.dynamic_index_in_dim(table_spread, my_table, keepdims=False)
    normed = (centred * lax.rsqrt(mine_spread + EPSILON)[None, :, None]).astype(jnp.bfloat16)
    normed_rows = lax.all_to_all(normed, "feat", split_axis=0, concat_axis=1, tiled=True)
    projected = jnp.dot(normed_rows, feat_qkv, preferred_element_type=jnp.float32).astype(
        jnp.bfloat16
    )
    queries = into_heads(projected[..., :width_all])
    key_part = into_heads(projected[..., width_all : 2 * width_all])
    value_part = into_heads(projected[..., 2 * width_all :])
    mixed_rows = feature_layer(normed_rows, feat_out, key_part, value_part, queries)
    group_rows, total_feats = (mixed_rows.shape[0], mixed_rows.shape[1])
    per_device = total_feats * HEADS // row_devices
    first_row = row_index * rows_here + feat_index * group_rows
    train_here = lax.dynamic_slice_in_dim(row_train, first_row, group_rows)
    places = compact_train(train_here)
    chosen = jnp.take(mixed_rows, places, axis=0)
    item_query = jnp.dot(
        mixed_rows, item_qkv[:, :width_all], preferred_element_type=jnp.float32
    ).astype(jnp.bfloat16)
    item_query = item_query.reshape(group_rows, row_devices, per_device, HEAD_DIM)
    key_value = jnp.dot(chosen, item_qkv[:, width_all:], preferred_element_type=jnp.float32).astype(
        jnp.bfloat16
    )
    item_key = key_value[..., :width_all].reshape(KEEP, row_devices, per_device, HEAD_DIM)
    item_value = key_value[..., width_all:].reshape(KEEP, row_devices, per_device, HEAD_DIM)
    query_table = jnp.repeat(block_table, group_rows)
    groups_all = row_train.reshape(row_devices, feat_devices, group_rows)
    group_counts = jnp.sum(groups_all, axis=2)
    slot_ids = jnp.arange(KEEP, dtype=jnp.int32)
    key_valid = slot_ids[None, None, :] < jnp.transpose(group_counts)[:, :, None]
    key_table = jnp.broadcast_to(block_table[None, :, None], key_valid.shape)
    allowed = (query_table[:, None] == key_table.reshape(-1)[None, :]) & key_valid.reshape(-1)[
        None, :
    ]
    query_count = query_table.shape[0]
    key_count = allowed.shape[1]
    query_blocks = max(1, query_count // 512)
    while query_count % query_blocks:
        query_blocks -= 1
    scaling = HEAD_DIM ** (-0.5)
    blocked_allowed = allowed.reshape(query_blocks, query_count // query_blocks, key_count)
    local_query = lax.all_to_all(item_query, "rows", split_axis=1, concat_axis=0, tiled=True)
    local_key = lax.all_to_all(item_key, "rows", split_axis=1, concat_axis=0, tiled=True)
    local_value = lax.all_to_all(item_value, "rows", split_axis=1, concat_axis=0, tiled=True)
    every_key, every_value = gather_together((local_key, local_value), "feat", (0, 0))

    def one_item(item_parts):
        single_query, single_key, single_value = item_parts

        def one_one_block(block_parts):
            block_query, block_allowed = block_parts
            scores = (
                jnp.dot(block_query, single_key.T, preferred_element_type=jnp.float32) * scaling
            )
            scores = jnp.where(block_allowed, scores, MASKED)
            shares = jax.nn.softmax(scores, axis=-1).astype(jnp.bfloat16)
            return jnp.dot(shares, single_value, preferred_element_type=jnp.float32).astype(
                jnp.bfloat16
            )

        blocked_query = single_query.reshape(query_blocks, query_count // query_blocks, HEAD_DIM)
        return lax.map(one_one_block, (blocked_query, blocked_allowed)).reshape(
            query_count, HEAD_DIM
        )

    by_item = (
        jnp.moveaxis(local_query[:, 0], 1, 0),
        jnp.moveaxis(every_key[:, 0], 1, 0),
        jnp.moveaxis(every_value[:, 0], 1, 0),
    )
    result = jnp.moveaxis(lax.map(one_item, by_item), 0, 1)[:, None]
    attended = lax.all_to_all(result, "rows", split_axis=0, concat_axis=1, tiled=True)
    attended = attended.reshape(group_rows, total_feats, width_all)
    update = jnp.dot(attended, item_out, preferred_element_type=jnp.float32)
    return (mixed_rows.astype(jnp.float32) + update).astype(jnp.bfloat16)


def solution(mesh):
    return jax.shard_map(
        on_device,
        mesh=mesh,
        in_specs=(P("rows", "feat", None), P(), P(), P(), P(), P(), P(), P()),
        out_specs=P(("rows", "feat"), None, None),
        check_vma=False,
    )
```

profile of v0, /device:TPU:1, one launch (start us, length us, event | category | flops | bytes accessed | tf_op | source)
XLA Modules:
  0.0 263.0 jit_solution(8148468147780909118)
XLA Ops:
  7.5 13.1 %all-to-all-start = ((f32[64,1,328]{2,1,0:T(1,128)}), f32[64,1,328]{2,1,0:T(1,128)S(1)}, u32[]{:S(2)}, u32[]{:S(2)}) async-start(f32[64,1,328]{2,1,0:T(1,128)} %broadcast_in_dim.81), calls=%async_computation | async-start | bytes 196608 | tf_op jit(solution)/shard_map/all_to_all | solution.py:16
  28.9 2.0 all-to-all-done
  32.7 4.0 %all-to-all-start.1 = ((bf16[128,20,128]{2,1,0:T(8,128)(2,1)}), bf16[128,20,128]{2,1,0:T(8,128)(2,1)S(1)}, u32[]{:S(2)}, u32[]{:S(2)}) async-start(bf16[128,20,128]{2,1,0:T(8,128)(2,1)} %fusion.31), calls=%async_computation.1 | async-start | bytes 1572864 | tf_op jit(solution)/shard_map/all_to_all | solution.py:127
  36.8 11.7 %all-to-all-done.1 = bf16[128,20,128]{2,1,0:T(8,128)(2,1)S(1)} async-done(((bf16[128,20,128]{2,1,0:T(8,128)(2,1)}), bf16[128,20,128]{2,1,0:T(8,128)(2,1)S(1)}, u32[]{:S(2)}, u32[]{:S(2)}) %all-to-all-start.1) | async-done | bytes 655392 | tf_op jit(solution)/shard_map/all_to_all | solution.py:127
  52.2 10.6 %while.32 = (s32[]{:T(128)}, bf16[2,16,80,4,32]{2,4,3,1,0:T(8,128)(2,1)}, bf16[2,16,80,4,32]{2,4,3,1,0:T(8,128)(2,1)}, bf16[2,16,80,4,32]{2,4,3,1,0:T(8,128)(2,1...) while((s32[]{:T(128)}, bf16[2,16,80,4,32]{2,4,3,1,0:T(8,128)(2,1)}, ...), condition=%wide.region_7.8_spmd, body=%wide.region_4.7_spmd.sunk | while | flops 55050320 | bytes 12310625 | solution.py:86
  52.8 3.4 %fusion.75 = (f32[16,4,80]{2,1,0:T(4,128)S(1)}, f32[16,4,80,80]{2,3,1,0:T(8,128)S(1)}) fusion(f32[16,4,80,80]{2,3,1,0:T(8,128)S(1)} %fusion.74), kind=kOutput, calls=%fused_computation.90.clone.1 | output fusion | flops 1638479 | bytes 3297280 | tf_op jit(solution)/shard_map/while/body/eval_jaxpr/sub | solution.py:78
  58.1 3.4 %fusion.75 = (f32[16,4,80]{2,1,0:T(4,128)S(1)}, f32[16,4,80,80]{2,3,1,0:T(8,128)S(1)}) fusion(f32[16,4,80,80]{2,3,1,0:T(8,128)S(1)} %fusion.74), kind=kOutput, calls=%fused_computation.90.clone.1 | output fusion | flops 1638479 | bytes 3297280 | tf_op jit(solution)/shard_map/while/body/eval_jaxpr/sub | solution.py:78
  62.8 1.7 fusion.32
  67.1 9.5 %all-to-all-start.3 = ((bf16[64,2,320]{2,1,0:T(2,128)(2,1)}), bf16[64,2,320]{2,1,0:T(2,128)(2,1)S(1)}, u32[]{:S(2)}, u32[]{:S(2)}) async-start(bf16[64,2,320]{2,1,0:T(2,128)(2,1)} %reshape.192), calls=%async_computation.3 | async-start | bytes 196608 | tf_op jit(solution)/shard_map/all_to_all | solution.py:167
  78.5 3.8 %reshape.164 = bf16[32,64,5,32]{3,2,1,0:T(8,128)(2,1)} reshape(bf16[32,80,128]{2,1,0:T(8,128)(2,1)S(1)} %convolution_convert_fusion.2) | data formatting | bytes 1310720 | tf_op jit(solution)/shard_map/reshape | solution.py:144
  82.4 5.2 %copy.144 = bf16[32,64,5,32]{3,0,2,1:T(8,128)(2,1)S(1)} copy(bf16[32,64,5,32]{3,2,1,0:T(8,128)(2,1)} %reshape.164) | data formatting | bytes 1310720 | tf_op jit(solution)/shard_map/reshape | solution.py:144
  87.6 2.6 reshape.188
  90.2 10.3 %all-to-all-start.4 = ((bf16[64,2,320]{2,1,0:T(2,128)(2,1)}), bf16[64,2,320]{2,1,0:T(2,128)(2,1)S(1)}, u32[]{:S(2)}, u32[]{:S(2)}) async-start(bf16[64,2,320]{2,1,0:T(2,128)(2,1)} %reshape.190), calls=%async_computation.4 | async-start | bytes 196608 | tf_op jit(solution)/shard_map/all_to_all | solution.py:168
  101.3 9.4 %all-to-all-done.4 = bf16[64,2,320]{2,1,0:T(2,128)(2,1)S(1)} async-done(((bf16[64,2,320]{2,1,0:T(2,128)(2,1)}), bf16[64,2,320]{2,1,0:T(2,128)(2,1)S(1)}, u32[]{:S(2)}, u32[]{:S(2)}) %all-to-all-start.4) | async-done | bytes 81952 | tf_op jit(solution)/shard_map/all_to_all | solution.py:168
  110.7 4.5 %all-to-all-start.2 = ((bf16[64,2,2560]{2,1,0:T(2,128)(2,1)}), bf16[64,2,2560]{2,1,0:T(2,128)(2,1)S(1)}, u32[]{:S(2)}, u32[]{:S(2)}) async-start(bf16[64,2,2560]{2,1,0:T(2,128)(2,1)} %reshape.188), calls=%async_computation.2 | async-start | bytes 1310720 | tf_op jit(solution)/shard_map/all_to_all | solution.py:166
  116.0 11.3 %all-gather = bf16[327680]{0:T(1024)(128)(2,1)S(1)} all-gather(bf16[81920]{0:T(1024)(128)(2,1)S(1)} %pad_maximum_fusion), channel_id=2, replica_groups=mesh['rows'=64,'feat'=4] {'feat'}, dimensions={0}, use_global_device_ids=true | all-gather | bytes 819200 | tf_op jit(solution)/shard_map/all_gather | solution.py:43
  128.4 2.3 squeeze_reshape_reshape.6
  136.7 2.0 bitcast_bitcast_fusion
  138.7 3.9 %copy.111 = bf16[64,32,1,5,32]{1,0,4,3,2:T(8,128)(2,1)S(1)} copy(bf16[64,32,1,5,32]{4,1,3,0,2:T(8,128)(2,1)} %bitcast_bitcast_fusion) | data formatting | bytes 1310720 | tf_op jit(solution)/shard_map/all_to_all | solution.py:166
  142.6 3.5 %squeeze.38 = bf16[2048,5,32]{0,2,1:T(8,128)(2,1)} reshape(bf16[64,32,1,5,32]{1,0,4,3,2:T(8,128)(2,1)S(1)} %copy.111) | data formatting | bytes 1310720 | tf_op jit(solution)/shard_map/squeeze | solution.py:191
  146.1 59.1 %while.34 = (s32[]{:T(128)}, bf16[5,2048,32]{2,1,0:T(8,128)(2,1)}, bf16[5,2048,32]{1,2,0:T(8,128)(2,1)}, bf16[5,1024,32]{2,1,0:T(8,128)(2,1)}, bf16[5,1024,32]{2...) while((s32[]{:T(128)}, bf16[5,2048,32]{2,1,0:T(8,128)(2,1)}, ...), condition=%wide.region_16.17_spmd.clone, body=%wide.region_11.16_spmd.clone.sunk | while | flops 75512832 | bytes 11330310 | solution.py:195
  149.9 6.9 %while.35 = (s32[]{:T(128)}, bf16[4,512,32]{1,2,0:T(8,128)(2,1)S(1)}, pred[4,512,1024]{2,1,0:T(32,128)(4,1)S(1)}, bf16[4,512,32]{2,1,0:T(8,128)(2,1)S(1)}, bf16[...) while((s32[]{:T(128)}, bf16[4,512,32]{1,2,0:T(8,128)(2,1)S(1)}, ...), condition=%wide.region_15.15_spmd, body=%wide.region_12.14_spmd.sunk | while | flops 71318528 | bytes 7515217 | solution.py:186
  161.7 6.9 %while.35 = (s32[]{:T(128)}, bf16[4,512,32]{1,2,0:T(8,128)(2,1)S(1)}, pred[4,512,1024]{2,1,0:T(32,128)(4,1)S(1)}, bf16[4,512,32]{2,1,0:T(8,128)(2,1)S(1)}, bf16[...) while((s32[]{:T(128)}, bf16[4,512,32]{1,2,0:T(8,128)(2,1)S(1)}, ...), condition=%wide.region_15.15_spmd, body=%wide.region_12.14_spmd.sunk | while | flops 71318528 | bytes 7515217 | solution.py:186
  173.5 6.9 %while.35 = (s32[]{:T(128)}, bf16[4,512,32]{1,2,0:T(8,128)(2,1)S(1)}, pred[4,512,1024]{2,1,0:T(32,128)(4,1)S(1)}, bf16[4,512,32]{2,1,0:T(8,128)(2,1)S(1)}, bf16[...) while((s32[]{:T(128)}, bf16[4,512,32]{1,2,0:T(8,128)(2,1)S(1)}, ...), condition=%wide.region_15.15_spmd, body=%wide.region_12.14_spmd.sunk | while | flops 71318528 | bytes 7515217 | solution.py:186
  185.4 6.9 %while.35 = (s32[]{:T(128)}, bf16[4,512,32]{1,2,0:T(8,128)(2,1)S(1)}, pred[4,512,1024]{2,1,0:T(32,128)(4,1)S(1)}, bf16[4,512,32]{2,1,0:T(8,128)(2,1)S(1)}, bf16[...) while((s32[]{:T(128)}, bf16[4,512,32]{1,2,0:T(8,128)(2,1)S(1)}, ...), condition=%wide.region_15.15_spmd, body=%wide.region_12.14_spmd.sunk | while | flops 71318528 | bytes 7515217 | solution.py:186
  197.2 6.9 %while.35 = (s32[]{:T(128)}, bf16[4,512,32]{1,2,0:T(8,128)(2,1)S(1)}, pred[4,512,1024]{2,1,0:T(32,128)(4,1)S(1)}, bf16[4,512,32]{2,1,0:T(8,128)(2,1)S(1)}, bf16[...) while((s32[]{:T(128)}, bf16[4,512,32]{1,2,0:T(8,128)(2,1)S(1)}, ...), condition=%wide.region_15.15_spmd, body=%wide.region_12.14_spmd.sunk | while | flops 71318528 | bytes 7515217 | solution.py:186
  205.2 5.1 %copy.143 = bf16[5,2048,32]{2,0,1:T(8,128)(2,1)} copy(bf16[5,2048,32]{2,1,0:T(8,128)(2,1)} %get-tuple-element.97) | data formatting | bytes 1310720 | tf_op jit(solution)/shard_map/while | solution.py:195
  210.3 5.4 %reshape.194 = bf16[64,2,2560]{2,1,0:T(2,128)(2,1)S(1)} reshape(bf16[2048,1,5,32]{3,2,1,0:T(8,128)(2,1)} %bitcast.147) | data formatting | bytes 1310720
  215.7 32.1 %all_to_all.84 = bf16[64,2,2560]{2,1,0:T(2,128)(2,1)S(1)} all-to-all(bf16[64,2,2560]{2,1,0:T(2,128)(2,1)S(1)} %reshape.194), channel_id=1, replica_groups=mesh['rows'=64,'feat'=4] {'rows'}, dimensions={0} | all-to-all | bytes 1310720 | tf_op jit(solution)/shard_map/all_to_all | solution.py:196
  247.8 4.0 %reshape.195 = bf16[2048,1,5,32]{3,2,1,0:T(8,128)(2,1)} reshape(bf16[64,2,2560]{2,1,0:T(2,128)(2,1)S(1)} %all_to_all.84) | data formatting | bytes 1310720
  251.8 5.3 %copy.142 = bf16[64,32,1,5,32]{4,3,0,1,2:T(8,128)(2,1)} copy(bf16[64,32,1,5,32]{4,3,1,0,2:T(8,128)(2,1)} %bitcast.148) | data formatting | bytes 1310720 | tf_op jit(solution)/shard_map/all_to_all | solution.py:196
  257.1 4.7 %reshape.171 = bf16[32,80,128]{2,1,0:T(8,128)(2,1)S(1)} reshape(bf16[32,64,1,5,32]{4,3,1,0,2:T(8,128)(2,1)} %bitcast.149) | data formatting | bytes 1310720 | tf_op jit(solution)/shard_map/reshape | solution.py:197
  (192 shorter events, 95.2 us)
Async XLA Ops:
  0.0 48.6 %copy-start = (bf16[128,384]{1,0:T(8,128)(2,1)S(1)}, bf16[128,384]{1,0:T(8,128)(2,1)}, u32[]{:S(2)}) copy-start(bf16[128,384]{1,0:T(8,128)(2,1)} %param.18) | copy-start | bytes 294916
  0.0 31.4 %copy-start.4 = (bf16[128,20,128]{2,0,1:T(8,128)(2,1)S(1)}, bf16[128,20,128]{2,0,1:T(8,128)(2,1)}, u32[]{:S(2)}) copy-start(bf16[128,20,128]{2,0,1:T(8,128)(2,1)} %param.14) | copy-start | bytes 1966084
  7.5 23.3 %all-to-all-start = ((f32[64,1,328]{2,1,0:T(1,128)}), f32[64,1,328]{2,1,0:T(1,128)S(1)}, u32[]{:S(2)}, u32[]{:S(2)}) async-start(f32[64,1,328]{2,1,0:T(1,128)} %broadcast_in_dim.81), calls=%async_computation | async-start | bytes 196608 | tf_op jit(solution)/shard_map/all_to_all | solution.py:16
  32.7 15.7 %all-to-all-start.1 = ((bf16[128,20,128]{2,1,0:T(8,128)(2,1)}), bf16[128,20,128]{2,1,0:T(8,128)(2,1)S(1)}, u32[]{:S(2)}, u32[]{:S(2)}) async-start(bf16[128,20,128]{2,1,0:T(8,128)(2,1)} %fusion.31), calls=%async_computation.1 | async-start | bytes 1572864 | tf_op jit(solution)/shard_map/all_to_all | solution.py:127
  52.2 10.6 %copy-start.7 = (bf16[128,128]{1,0:T(8,128)(2,1)S(1)}, bf16[128,128]{1,0:T(8,128)(2,1)}, u32[]{:S(2)}) copy-start(bf16[128,128]{1,0:T(8,128)(2,1)} %param.19) | copy-start | bytes 98308
  52.8 3.4 %copy-start.5 = (bf16[2,16,80,4,32]{2,4,3,1,0:T(8,128)(2,1)S(1)}, bf16[2,16,80,4,32]{2,4,3,1,0:T(8,128)(2,1)}, u32[]{:S(2)}) copy-start(bf16[2,16,80,4,32]{2,4,3,1,0:T(8,128)(2,1)} %get-tuple-element.407) | copy-start | bytes 1966084 | tf_op jit(solution)/shard_map/while
  58.1 3.4 %copy-start.5 = (bf16[2,16,80,4,32]{2,4,3,1,0:T(8,128)(2,1)S(1)}, bf16[2,16,80,4,32]{2,4,3,1,0:T(8,128)(2,1)}, u32[]{:S(2)}) copy-start(bf16[2,16,80,4,32]{2,4,3,1,0:T(8,128)(2,1)} %get-tuple-element.407) | copy-start | bytes 1966084 | tf_op jit(solution)/shard_map/while
  62.8 2.3 copy-start.6
  64.6 13.6 %copy-start.2 = (bf16[32,80,128]{2,1,0:T(8,128)(2,1)}, bf16[32,80,128]{2,1,0:T(8,128)(2,1)S(1)}, u32[]{:S(2)}) copy-start(bf16[32,80,128]{2,1,0:T(8,128)(2,1)S(1)} %fusion.32) | copy-start | bytes 1966084
  67.1 23.1 %all-to-all-start.3 = ((bf16[64,2,320]{2,1,0:T(2,128)(2,1)}), bf16[64,2,320]{2,1,0:T(2,128)(2,1)S(1)}, u32[]{:S(2)}, u32[]{:S(2)}) async-start(bf16[64,2,320]{2,1,0:T(2,128)(2,1)} %reshape.192), calls=%async_computation.3 | async-start | bytes 196608 | tf_op jit(solution)/shard_map/all_to_all | solution.py:167
  90.2 20.5 %all-to-all-start.4 = ((bf16[64,2,320]{2,1,0:T(2,128)(2,1)}), bf16[64,2,320]{2,1,0:T(2,128)(2,1)S(1)}, u32[]{:S(2)}, u32[]{:S(2)}) async-start(bf16[64,2,320]{2,1,0:T(2,128)(2,1)} %reshape.190), calls=%async_computation.4 | async-start | bytes 196608 | tf_op jit(solution)/shard_map/all_to_all | solution.py:168
  110.7 24.6 %all-to-all-start.2 = ((bf16[64,2,2560]{2,1,0:T(2,128)(2,1)}), bf16[64,2,2560]{2,1,0:T(2,128)(2,1)S(1)}, u32[]{:S(2)}, u32[]{:S(2)}) async-start(bf16[64,2,2560]{2,1,0:T(2,128)(2,1)} %reshape.188), calls=%async_computation.2 | async-start | bytes 1310720 | tf_op jit(solution)/shard_map/all_to_all | solution.py:166
  257.1 4.7 %copy-start.3 = (bf16[32,80,128]{2,1,0:T(8,128)(2,1)S(1)}, bf16[32,80,128]{2,1,0:T(8,128)(2,1)}, u32[]{:S(2)}) copy-start(bf16[32,80,128]{2,1,0:T(8,128)(2,1)} %copy-done.2) | copy-start | bytes 1966084
  257.1 4.7 %copy-start.8 = (bf16[128,128]{1,0:T(8,128)(2,1)S(1)}, bf16[128,128]{1,0:T(8,128)(2,1)}, u32[]{:S(2)}) copy-start(bf16[128,128]{1,0:T(8,128)(2,1)} %param.21) | copy-start | bytes 98308
  257.1 5.9 %copy-start.1 = (bf16[128,384]{1,0:T(8,128)(2,1)S(1)}, bf16[128,384]{1,0:T(8,128)(2,1)}, u32[]{:S(2)}) copy-start(bf16[128,384]{1,0:T(8,128)(2,1)} %param.18) | copy-start | bytes 294916
where the time goes:
time: 264 us; the launch traced here: 263 us
  local copies, waits for them, and re-layouts  85.9 us (33%)
  blocking collectives  43.3 us (16%)
  starting transfers between devices  41.4 us (16%)
  other arithmetic  33.3 us (13%)
  matrix products  31.7 us (12%)
  waiting for transfers between devices  23.7 us (9%)
  between operations  3.17 us (1%)
    all_to_all x1, blocking collectives, on_device(): lax.all_to_all(result, 'rows', split_axis=0, concat_axis=1, tiled=True)  32.1 us
    unnamed x26, local copies, waits for them, and re-layouts  18.4 us
    all_to_all x1, starting transfers between devices, from_everyone(): lax.all_to_all(jnp.broadcast_to(shard[None], (peers, *shard.shape)), axis...  13.1 us
    dot_general x20, matrix products, one_one_block(): jnp.dot(block_query, single_key.T, preferred_element_type=jnp.float32)  12 us
    dot_general x20, matrix products, one_one_block(): jnp.dot(shares, single_value, preferred_element_type=jnp.float32)  12 us
    all_to_all x1, waiting for transfers between devices, on_device(): lax.all_to_all(normed, 'feat', split_axis=0, concat_axis=1, tiled=True)  11.7 us
    all_gather x1, blocking collectives, gather_together(): lines, at, done = (lax.all_gather(vector, axis), 0, [])  11.3 us
    reduce_sum x20, other arithmetic, one_one_block(): shares = jax.nn.softmax(scores, axis=-1).astype(jnp.bfloat16)  10.3 us
  transfers between devices with their start and end apart: 5, of which 4 were waited for; matrix products, arithmetic and copies ran while one was open for 11% of the time, Pallas kernels for 0%

commit v1 on v0

--- a/solution.py
+++ b/solution.py
@@ -193,7 +193,10 @@
         jnp.moveaxis(every_value[:, 0], 1, 0),
     )
     result = jnp.moveaxis(lax.map(one_item, by_item), 0, 1)[:, None]
-    attended = lax.all_to_all(result, "rows", split_axis=0, concat_axis=1, tiled=True)
+    attended = jnp.concatenate(
+        lax.all_to_all(jnp.stack(jnp.split(result, lax.axis_size("rows"), axis=0)), "rows", 0, 0),
+        axis=1,
+    )
     attended = attended.reshape(group_rows, total_feats, width_all)
     update = jnp.dot(attended, item_out, preferred_element_type=jnp.float32)
     return (mixed_rows.astype(jnp.float32) + update).astype(jnp.bfloat16)

time: 264 us -> 282 us (1.068)
  local copies, waits for them, and re-layouts: 85.9 us -> 101 us
    unnamed x26 -> x89, local copies, waits for them, and re-layouts: 18.4 us -> 40.2 us
    all_to_all x1 -> x0, local copies, waits for them, and re-layouts: 5.32 us -> none  [on_device(): lax.all_to_all(result, 'rows', split_axis=0, concat_axis=1, tiled=True)]
    while x5 -> x4, local copies, waits for them, and re-layouts: 5.07 us -> 0.01 us  [the longest x1 5.06 us: on_device(): result = jnp.moveaxis(lax.map(one_item, by_item), 0, 1)[:, None]]
    another operation x2 -> x4, local copies, waits for them, and re-layouts: 0.86 us -> 5.56 us  [the longest x1 4.69 us: on_device(): attended = attended.reshape(group_rows, total_feats, width_all)]
  transfers between devices with their start and end apart: 5 -> 5, of which waited for: 4 -> 4; matrix products, arithmetic and copies ran while one was open for 11% -> 10% of each run, Pallas kernels for 0% -> 0%
where the time goes in v1:
time: 282 us; the launch traced here: 279 us
  local copies, waits for them, and re-layouts  101 us (36%)
  blocking collectives  43.2 us (15%)
  starting transfers between devices  41.3 us (15%)
  other arithmetic  34.3 us (12%)
  matrix products  31.7 us (11%)
  waiting for transfers between devices  23.8 us (8%)
  between operations  3.23 us (1%)
    unnamed x89, local copies, waits for them, and re-layouts  40.2 us
    all_to_all x1, blocking collectives, on_device(): lax.all_to_all(jnp.stack(jnp.split(result, lax.axis_size('rows'), axis=0)...  31.9 us
    all_to_all x1, starting transfers between devices, from_everyone(): lax.all_to_all(jnp.broadcast_to(shard[None], (peers, *shard.shape)), axis...  13.1 us
    dot_general x20, matrix products, one_one_block(): jnp.dot(block_query, single_key.T, preferred_element_type=jnp.float32)  12 us
    dot_general x20, matrix products, one_one_block(): jnp.dot(shares, single_value, preferred_element_type=jnp.float32)  12 us
    all_to_all x1, waiting for transfers between devices, on_device(): lax.all_to_all(normed, 'feat', split_axis=0, concat_axis=1, tiled=True)  11.7 us
    all_gather x1, blocking collectives, gather_together(): lines, at, done = (lax.all_gather(vector, axis), 0, [])  11.3 us
    all_to_all x1, starting transfers between devices, on_device(): lax.all_to_all(item_value, 'rows', split_axis=1, concat_axis=0, tiled=True)  10.3 us
  transfers between devices with their start and end apart: 5, of which 4 were waited for; matrix products, arithmetic and copies ran while one was open for 10% of the time, Pallas kernels for 0%

profile of v1, /device:TPU:1, one launch (start us, length us, event | category | flops | bytes accessed | tf_op | source)
XLA Modules:
  0.0 278.9 jit_solution(13271201226486438464)
XLA Ops:
  3.4 1.7 fusion.27
  7.4 13.1 %all-to-all-start = ((f32[64,1,328]{2,1,0:T(1,128)}), f32[64,1,328]{2,1,0:T(1,128)S(1)}, u32[]{:S(2)}, u32[]{:S(2)}) async-start(f32[64,1,328]{2,1,0:T(1,128)} %broadcast_in_dim.52), calls=%async_computation | async-start | bytes 196608 | tf_op jit(solution)/shard_map/all_to_all | solution.py:16
  28.5 2.2 all-to-all-done
  31.2 2.4 fusion.31
  33.7 4.0 %all-to-all-start.1 = ((bf16[128,20,128]{2,1,0:T(8,128)(2,1)}), bf16[128,20,128]{2,1,0:T(8,128)(2,1)S(1)}, u32[]{:S(2)}, u32[]{:S(2)}) async-start(bf16[128,20,128]{2,1,0:T(8,128)(2,1)} %fusion.31), calls=%async_computation.1 | async-start | bytes 1572864 | tf_op jit(solution)/shard_map/all_to_all | solution.py:127
  37.7 11.7 %all-to-all-done.1 = bf16[128,20,128]{2,1,0:T(8,128)(2,1)S(1)} async-done(((bf16[128,20,128]{2,1,0:T(8,128)(2,1)}), bf16[128,20,128]{2,1,0:T(8,128)(2,1)S(1)}, u32[]{:S(2)}, u32[]{:S(2)}) %all-to-all-start.1) | async-done | bytes 655392 | tf_op jit(solution)/shard_map/all_to_all | solution.py:127
  53.2 10.6 %while.32 = (s32[]{:T(128)}, bf16[2,16,80,4,32]{2,4,3,1,0:T(8,128)(2,1)}, bf16[2,16,80,4,32]{2,4,3,1,0:T(8,128)(2,1)}, bf16[2,16,80,4,32]{2,4,3,1,0:T(8,128)(2,1...) while((s32[]{:T(128)}, bf16[2,16,80,4,32]{2,4,3,1,0:T(8,128)(2,1)}, ...), condition=%wide.region_7.8_spmd, body=%wide.region_4.7_spmd.sunk | while | flops 55050320 | bytes 12310625 | solution.py:86
  53.7 3.4 %fusion.75 = (f32[16,4,80]{2,1,0:T(4,128)S(1)}, f32[16,4,80,80]{2,3,1,0:T(8,128)S(1)}) fusion(f32[16,4,80,80]{2,3,1,0:T(8,128)S(1)} %fusion.74), kind=kOutput, calls=%fused_computation.216.clone.1 | output fusion | flops 1638479 | bytes 3297280 | tf_op jit(solution)/shard_map/while/body/eval_jaxpr/sub | solution.py:78
  59.0 3.4 %fusion.75 = (f32[16,4,80]{2,1,0:T(4,128)S(1)}, f32[16,4,80,80]{2,3,1,0:T(8,128)S(1)}) fusion(f32[16,4,80,80]{2,3,1,0:T(8,128)S(1)} %fusion.74), kind=kOutput, calls=%fused_computation.216.clone.1 | output fusion | flops 1638479 | bytes 3297280 | tf_op jit(solution)/shard_map/while/body/eval_jaxpr/sub | solution.py:78
  68.0 9.3 %all-to-all-start.3 = ((bf16[64,2,320]{2,1,0:T(2,128)(2,1)}), bf16[64,2,320]{2,1,0:T(2,128)(2,1)S(1)}, u32[]{:S(2)}, u32[]{:S(2)}) async-start(bf16[64,2,320]{2,1,0:T(2,128)(2,1)} %reshape.319), calls=%async_computation.3 | async-start | bytes 196608 | tf_op jit(solution)/shard_map/all_to_all | solution.py:167
  79.3 3.8 %reshape.291 = bf16[32,64,5,32]{3,2,1,0:T(8,128)(2,1)} reshape(bf16[32,80,128]{2,1,0:T(8,128)(2,1)S(1)} %convolution_convert_fusion.2) | data formatting | bytes 1310720 | tf_op jit(solution)/shard_map/reshape | solution.py:144
  83.0 5.2 %copy.137 = bf16[32,64,5,32]{3,0,2,1:T(8,128)(2,1)S(1)} copy(bf16[32,64,5,32]{3,2,1,0:T(8,128)(2,1)} %reshape.291) | data formatting | bytes 1310720 | tf_op jit(solution)/shard_map/reshape | solution.py:144
  88.3 2.6 reshape.315
  90.9 10.3 %all-to-all-start.4 = ((bf16[64,2,320]{2,1,0:T(2,128)(2,1)}), bf16[64,2,320]{2,1,0:T(2,128)(2,1)S(1)}, u32[]{:S(2)}, u32[]{:S(2)}) async-start(bf16[64,2,320]{2,1,0:T(2,128)(2,1)} %reshape.317), calls=%async_computation.4 | async-start | bytes 196608 | tf_op jit(solution)/shard_map/all_to_all | solution.py:168
  102.0 9.4 %all-to-all-done.4 = bf16[64,2,320]{2,1,0:T(2,128)(2,1)S(1)} async-done(((bf16[64,2,320]{2,1,0:T(2,128)(2,1)}), bf16[64,2,320]{2,1,0:T(2,128)(2,1)S(1)}, u32[]{:S(2)}, u32[]{:S(2)}) %all-to-all-start.4) | async-done | bytes 81952 | tf_op jit(solution)/shard_map/all_to_all | solution.py:168
  111.4 4.5 %all-to-all-start.2 = ((bf16[64,2,2560]{2,1,0:T(2,128)(2,1)}), bf16[64,2,2560]{2,1,0:T(2,128)(2,1)S(1)}, u32[]{:S(2)}, u32[]{:S(2)}) async-start(bf16[64,2,2560]{2,1,0:T(2,128)(2,1)} %reshape.315), calls=%async_computation.2 | async-start | bytes 1310720 | tf_op jit(solution)/shard_map/all_to_all | solution.py:166
  116.6 11.3 %all-gather = bf16[327680]{0:T(1024)(128)(2,1)S(1)} all-gather(bf16[81920]{0:T(1024)(128)(2,1)S(1)} %pad_maximum_fusion), channel_id=2, replica_groups=mesh['rows'=64,'feat'=4] {'feat'}, dimensions={0}, use_global_device_ids=true | all-gather | bytes 819200 | tf_op jit(solution)/shard_map/all_gather | solution.py:43
  129.1 2.3 squeeze_reshape_reshape.6
  137.4 2.0 bitcast_bitcast_fusion.1
  139.3 3.9 %copy.109 = bf16[64,32,1,5,32]{1,0,4,3,2:T(8,128)(2,1)S(1)} copy(bf16[64,32,1,5,32]{4,1,3,0,2:T(8,128)(2,1)} %bitcast_bitcast_fusion.1) | data formatting | bytes 1310720 | tf_op jit(solution)/shard_map/all_to_all | solution.py:166
  143.2 3.5 %squeeze.38 = bf16[2048,5,32]{0,2,1:T(8,128)(2,1)} reshape(bf16[64,32,1,5,32]{1,0,4,3,2:T(8,128)(2,1)S(1)} %copy.109) | data formatting | bytes 1310720 | tf_op jit(solution)/shard_map/squeeze | solution.py:191
  146.7 59.1 %while.34 = (s32[]{:T(128)}, bf16[5,2048,32]{2,1,0:T(8,128)(2,1)}, bf16[5,2048,32]{1,2,0:T(8,128)(2,1)}, bf16[5,1024,32]{2,1,0:T(8,128)(2,1)}, bf16[5,1024,32]{2...) while((s32[]{:T(128)}, bf16[5,2048,32]{2,1,0:T(8,128)(2,1)}, ...), condition=%wide.region_16.17_spmd.clone, body=%wide.region_11.16_spmd.clone.sunk | while | flops 75512832 | bytes 11330310 | solution.py:195
  150.5 6.9 %while.35 = (s32[]{:T(128)}, bf16[4,512,32]{1,2,0:T(8,128)(2,1)S(1)}, pred[4,512,1024]{2,1,0:T(32,128)(4,1)S(1)}, bf16[4,512,32]{2,1,0:T(8,128)(2,1)S(1)}, bf16[...) while((s32[]{:T(128)}, bf16[4,512,32]{1,2,0:T(8,128)(2,1)S(1)}, ...), condition=%wide.region_15.15_spmd, body=%wide.region_12.14_spmd.sunk | while | flops 71318528 | bytes 7515217 | solution.py:186
  162.4 6.9 %while.35 = (s32[]{:T(128)}, bf16[4,512,32]{1,2,0:T(8,128)(2,1)S(1)}, pred[4,512,1024]{2,1,0:T(32,128)(4,1)S(1)}, bf16[4,512,32]{2,1,0:T(8,128)(2,1)S(1)}, bf16[...) while((s32[]{:T(128)}, bf16[4,512,32]{1,2,0:T(8,128)(2,1)S(1)}, ...), condition=%wide.region_15.15_spmd, body=%wide.region_12.14_spmd.sunk | while | flops 71318528 | bytes 7515217 | solution.py:186
  174.2 6.9 %while.35 = (s32[]{:T(128)}, bf16[4,512,32]{1,2,0:T(8,128)(2,1)S(1)}, pred[4,512,1024]{2,1,0:T(32,128)(4,1)S(1)}, bf16[4,512,32]{2,1,0:T(8,128)(2,1)S(1)}, bf16[...) while((s32[]{:T(128)}, bf16[4,512,32]{1,2,0:T(8,128)(2,1)S(1)}, ...), condition=%wide.region_15.15_spmd, body=%wide.region_12.14_spmd.sunk | while | flops 71318528 | bytes 7515217 | solution.py:186
  186.0 6.9 %while.35 = (s32[]{:T(128)}, bf16[4,512,32]{1,2,0:T(8,128)(2,1)S(1)}, pred[4,512,1024]{2,1,0:T(32,128)(4,1)S(1)}, bf16[4,512,32]{2,1,0:T(8,128)(2,1)S(1)}, bf16[...) while((s32[]{:T(128)}, bf16[4,512,32]{1,2,0:T(8,128)(2,1)S(1)}, ...), condition=%wide.region_15.15_spmd, body=%wide.region_12.14_spmd.sunk | while | flops 71318528 | bytes 7515217 | solution.py:186
  197.9 6.9 %while.35 = (s32[]{:T(128)}, bf16[4,512,32]{1,2,0:T(8,128)(2,1)S(1)}, pred[4,512,1024]{2,1,0:T(32,128)(4,1)S(1)}, bf16[4,512,32]{2,1,0:T(8,128)(2,1)S(1)}, bf16[...) while((s32[]{:T(128)}, bf16[4,512,32]{1,2,0:T(8,128)(2,1)S(1)}, ...), condition=%wide.region_15.15_spmd, body=%wide.region_12.14_spmd.sunk | while | flops 71318528 | bytes 7515217 | solution.py:186
  231.7 1.9 reshape.321
  233.7 31.9 %all_to_all.74 = bf16[64,2,2560]{2,1,0:T(2,128)(2,1)} all-to-all(bf16[64,2,2560]{2,1,0:T(2,128)(2,1)S(1)} %reshape.321), channel_id=1, replica_groups=mesh['rows'=64,'feat'=4] {'rows'}, dimensions={0} | all-to-all | bytes 1310720 | tf_op jit(solution)/shard_map/all_to_all | solution.py:197
  265.6 3.6 %reshape.322 = bf16[64,1,5,32,32]{4,3,2,1,0:T(8,128)(2,1)S(1)} reshape(bf16[64,2,2560]{2,1,0:T(2,128)(2,1)} %all_to_all.74) | data formatting | bytes 1310720
  269.7 3.3 %copy.119 = bf16[32,64,1,5,32]{4,3,1,0,2:T(8,128)(2,1)} copy(bf16[32,64,1,5,32]{4,0,3,2,1:T(8,128)(2,1)S(1)} %bitcast_bitcast_fusion) | data formatting | bytes 1310720 | tf_op jit(solution)/shard_map/reshape | solution.py:196
  273.0 4.7 %reshape_reshape.15 = bf16[32,80,128]{2,1,0:T(8,128)(2,1)S(1)} reshape(bf16[32,64,1,5,32]{4,3,1,0,2:T(8,128)(2,1)} %copy.119) | data formatting | bytes 1310720 | tf_op jit(solution)/shard_map/reshape;reshape | solution.py:200
  (256 shorter events, 119.7 us)
Async XLA Ops:
  0.0 49.5 %copy-start = (bf16[128,384]{1,0:T(8,128)(2,1)S(1)}, bf16[128,384]{1,0:T(8,128)(2,1)}, u32[]{:S(2)}) copy-start(bf16[128,384]{1,0:T(8,128)(2,1)} %param.18) | copy-start | bytes 294916
  7.4 23.3 %all-to-all-start = ((f32[64,1,328]{2,1,0:T(1,128)}), f32[64,1,328]{2,1,0:T(1,128)S(1)}, u32[]{:S(2)}, u32[]{:S(2)}) async-start(f32[64,1,328]{2,1,0:T(1,128)} %broadcast_in_dim.52), calls=%async_computation | async-start | bytes 196608 | tf_op jit(solution)/shard_map/all_to_all | solution.py:16
  33.7 15.7 %all-to-all-start.1 = ((bf16[128,20,128]{2,1,0:T(8,128)(2,1)}), bf16[128,20,128]{2,1,0:T(8,128)(2,1)S(1)}, u32[]{:S(2)}, u32[]{:S(2)}) async-start(bf16[128,20,128]{2,1,0:T(8,128)(2,1)} %fusion.31), calls=%async_computation.1 | async-start | bytes 1572864 | tf_op jit(solution)/shard_map/all_to_all | solution.py:127
  53.1 10.6 %copy-start.7 = (bf16[128,128]{1,0:T(8,128)(2,1)S(1)}, bf16[128,128]{1,0:T(8,128)(2,1)}, u32[]{:S(2)}) copy-start(bf16[128,128]{1,0:T(8,128)(2,1)} %param.19) | copy-start | bytes 98308
  53.1 12.9 %copy-start.6 = (bf16[128,384]{1,0:T(8,128)(2,1)S(1)}, bf16[128,384]{1,0:T(8,128)(2,1)}, u32[]{:S(2)}) copy-start(bf16[128,384]{1,0:T(8,128)(2,1)} %param.20) | copy-start | bytes 294916
  53.7 3.4 %copy-start.5 = (bf16[2,16,80,4,32]{2,4,3,1,0:T(8,128)(2,1)S(1)}, bf16[2,16,80,4,32]{2,4,3,1,0:T(8,128)(2,1)}, u32[]{:S(2)}) copy-start(bf16[2,16,80,4,32]{2,4,3,1,0:T(8,128)(2,1)} %get-tuple-element.407) | copy-start | bytes 1966084 | tf_op jit(solution)/shard_map/while
  59.0 3.4 %copy-start.5 = (bf16[2,16,80,4,32]{2,4,3,1,0:T(8,128)(2,1)S(1)}, bf16[2,16,80,4,32]{2,4,3,1,0:T(8,128)(2,1)}, u32[]{:S(2)}) copy-start(bf16[2,16,80,4,32]{2,4,3,1,0:T(8,128)(2,1)} %get-tuple-element.407) | copy-start | bytes 1966084 | tf_op jit(solution)/shard_map/while
  65.4 13.8 %copy-start.2 = (bf16[32,80,128]{2,1,0:T(8,128)(2,1)}, bf16[32,80,128]{2,1,0:T(8,128)(2,1)S(1)}, u32[]{:S(2)}) copy-start(bf16[32,80,128]{2,1,0:T(8,128)(2,1)S(1)} %fusion.32) | copy-start | bytes 1966084
  68.0 22.9 %all-to-all-start.3 = ((bf16[64,2,320]{2,1,0:T(2,128)(2,1)}), bf16[64,2,320]{2,1,0:T(2,128)(2,1)S(1)}, u32[]{:S(2)}, u32[]{:S(2)}) async-start(bf16[64,2,320]{2,1,0:T(2,128)(2,1)} %reshape.319), calls=%async_computation.3 | async-start | bytes 196608 | tf_op jit(solution)/shard_map/all_to_all | solution.py:167
  90.9 20.5 %all-to-all-start.4 = ((bf16[64,2,320]{2,1,0:T(2,128)(2,1)}), bf16[64,2,320]{2,1,0:T(2,128)(2,1)S(1)}, u32[]{:S(2)}, u32[]{:S(2)}) async-start(bf16[64,2,320]{2,1,0:T(2,128)(2,1)} %reshape.317), calls=%async_computation.4 | async-start | bytes 196608 | tf_op jit(solution)/shard_map/all_to_all | solution.py:168
  111.4 24.6 %all-to-all-start.2 = ((bf16[64,2,2560]{2,1,0:T(2,128)(2,1)}), bf16[64,2,2560]{2,1,0:T(2,128)(2,1)S(1)}, u32[]{:S(2)}, u32[]{:S(2)}) async-start(bf16[64,2,2560]{2,1,0:T(2,128)(2,1)} %reshape.315), calls=%async_computation.2 | async-start | bytes 1310720 | tf_op jit(solution)/shard_map/all_to_all | solution.py:166
  205.9 25.4 %copy-start.4 = (bf16[5,2048,32]{2,1,0:T(8,128)(2,1)S(1)}, bf16[5,2048,32]{2,1,0:T(8,128)(2,1)}, u32[]{:S(2)}) copy-start(bf16[5,2048,32]{2,1,0:T(8,128)(2,1)} %get-tuple-element.97) | copy-start | bytes 1966084
  269.7 9.2 %copy-start.1 = (bf16[128,384]{1,0:T(8,128)(2,1)S(1)}, bf16[128,384]{1,0:T(8,128)(2,1)}, u32[]{:S(2)}) copy-start(bf16[128,384]{1,0:T(8,128)(2,1)} %param.18) | copy-start | bytes 294916
  273.0 4.7 %copy-start.3 = (bf16[32,80,128]{2,1,0:T(8,128)(2,1)S(1)}, bf16[32,80,128]{2,1,0:T(8,128)(2,1)}, u32[]{:S(2)}) copy-start(bf16[32,80,128]{2,1,0:T(8,128)(2,1)} %copy-done.2) | copy-start | bytes 1966084
  273.0 4.7 %copy-start.8 = (bf16[128,128]{1,0:T(8,128)(2,1)S(1)}, bf16[128,128]{1,0:T(8,128)(2,1)}, u32[]{:S(2)}) copy-start(bf16[128,128]{1,0:T(8,128)(2,1)} %param.21) | copy-start | bytes 98308
